TPU v7x, 768 devices: a whole 4x8x12 slice. The times are simulated.
768 devices in a mesh: section: 48 (over y_lo, z, core), tensor: 4 (over y_hi), dp: 4 (over x).
Axes of the slice: x: 4, y: 8 (y_hi: 4, y_lo: 2; y = y_hi * 2 + y_lo), z: 12, core: 2. Of those that a mesh axis runs over, the one named last changes fastest.
Arguments:
- hidden: bfloat16 [1536, 8192], P(('section', 'dp'), 'tensor'), may hold values from -250 to 250
- vocab_weight: bfloat16 [8192, 122880], P(None, ('section', 'tensor')), may hold values from -0.6 to 0.6
- target_ids: int32 [1536], P(('section', 'dp')), may hold values from 0 to 122879
- ref_logp: float32 [1536], P(('section', 'dp')), may hold values from -8 to -0.5
- response_lengths: int32 [192], P(('section', 'dp')), may hold values from 1 to 8
Outputs:
- token_logp: float32 [1536], P(('section', 'dp'))
- entropy: float32 [1536], P(('section', 'dp'))
- kl_term: float32 [1536], P(('section', 'dp'))
All inputs are finite; a program needn't handle non-finite values.
Results may differ from a plain program's by a relative error of at most 0.0015.
Values may be sent and summed in bfloat16 or wider, within the bound.
No kernel may reach another device: no remote copies, remote signals or barrier semaphores. Data moves between devices by JAX's collectives and lax.ppermute only.
A program may use at most 64 MiB of HBM per device.

v0:
```python
import jax
import jax.numpy as jnp
from jax import lax
from jax.sharding import PartitionSpec as P


def joined(part, axis, combine):
    gathered = jax.tree.map(lambda a: lax.all_gather(a, axis), part)

    def take(source):
        return jax.tree.map(lambda a: lax.dynamic_index_in_dim(a, source, 0, False), gathered)

    return lax.fori_loop(
        1, lax.axis_size(axis), lambda source, state: combine(state, take(source)), take(0)
    )


def combine(first, second):
    top = jnp.maximum(first[0], second[0])
    left = jnp.exp(first[0] - top)
    right = jnp.exp(second[0] - top)
    return (
        top,
        first[1] * left + second[1] * right,
        first[2] * left + second[2] * right,
        first[3] + second[3],
    )


def per_device(hidden, vocab_weight, target_ids, ref_logp, response_lengths):
    row_dev = hidden.shape[0]
    voc_dev = vocab_weight.shape[1]
    whole = lax.all_gather(hidden, "tensor", axis=1, tiled=True)
    logits = jnp.dot(
        lax.all_gather(whole, "section", axis=0, tiled=True),
        vocab_weight,
        preferred_element_type=jnp.float32,
    )
    all_ids = lax.all_gather(target_ids, "section", axis=0, tiled=True)
    offset = (
        lax.axis_index("section") * lax.axis_size("tensor") + lax.axis_index("tensor")
    ) * voc_dev
    top = jnp.max(logits, axis=1)
    expo = jnp.exp(logits - top[:, None])
    total = jnp.sum(expo, axis=1)
    moment = jnp.sum(expo * logits, axis=1)
    column = offset + jnp.arange(voc_dev, dtype=jnp.int32)
    picked = jnp.sum(jnp.where(all_ids[:, None] == column[None, :], logits, 0.0), axis=1)
    merged = joined((top, total, moment, picked), ("section", "tensor"), combine)
    begin = lax.axis_index("section") * row_dev
    top_own, total_own, moment_own, picked_own = [
        lax.dynamic_slice_in_dim(item, begin, row_dev, 0) for item in merged
    ]
    lse = top_own + jnp.log(total_own)
    logp = picked_own - lse
    ent = lse - moment_own / total_own
    slot = jnp.arange(row_dev, dtype=jnp.int32)
    live = (slot < response_lengths[0]).astype(jnp.float32)
    return (logp * live, ent * live, (logp - ref_logp) * live)


def solution(mesh):
    in_specs = (
        P(("section", "dp"), "tensor"),
        P(None, ("section", "tensor")),
        P(("section", "dp")),
        P(("section", "dp")),
        P(("section", "dp")),
    )
    out_specs = (P(("section", "dp")), P(("section", "dp")), P(("section", "dp")))
    return jax.shard_map(
        per_device, mesh=mesh, in_specs=in_specs, out_specs=out_specs, check_vma=False
    )
```

profile of v0, /device:TPU:26, one launch (start us, length us, event | category | flops | bytes accessed | tf_op | source)
XLA Modules:
  0.0 1991.0 jit_solution(17989487404388168082)
XLA Ops:
  7.2 0.0 all-gather.10.cloned.1.call-start
  7.2 15.0 all_gather.33
  22.2 0.0 all-gather.10.cloned.1.call-update
  22.9 1.3 dynamic-slice
  24.8 0.9 dynamic-update-slice
  25.7 90.1 %all-reduce = s32[384]{0:T(512)S(1)} all-reduce(s32[384]{0:T(512)S(1)} %dynamic-update-slice), channel_id=1, replica_groups=mesh['section'=48,'tensor'=4,'dp'=4] {'section'}, use_global_device_ids=true, to_apply=%add | all-reduce | flops 384 | bytes 3072
  115.8 0.0 copy-start
  115.8 14.0 all-gather.10.cloned.1.call-done
  129.9 12.5 fusion.2
  142.4 451.6 %all-gather.4 = f32[192,1,384]{2,1,0:T(1,128)S(1)} all-gather(f32[1,1,384]{2,1,0:T(1,128)S(1)} %reshape.27), channel_id=2, replica_groups=mesh['section'=48,'tensor'=4,'dp'=4] {'section','tensor'}, dimensions={0}, use_global_device_ids=true | all-gather | bytes 296448 | tf_op jit(solution)/shard_map/all_gather | solution.py:8
  594.1 0.5 multiply_reduce_fusion
  594.6 456.0 %all-gather.5 = f32[192,1,384]{2,1,0:T(1,128)S(1)} all-gather(f32[1,1,384]{2,1,0:T(1,128)S(1)} %reshape.29), channel_id=3, replica_groups=mesh['section'=48,'tensor'=4,'dp'=4] {'section','tensor'}, dimensions={0}, use_global_device_ids=true | all-gather | bytes 296448 | tf_op jit(solution)/shard_map/all_gather | solution.py:8
  1050.7 451.1 %all-gather.6 = f32[192,1,384]{2,1,0:T(1,128)S(1)} all-gather(f32[1,1,384]{2,1,0:T(1,128)S(1)} %reshape.31), channel_id=4, replica_groups=mesh['section'=48,'tensor'=4,'dp'=4] {'section','tensor'}, dimensions={0}, use_global_device_ids=true | all-gather | bytes 296448 | tf_op jit(solution)/shard_map/all_gather | solution.py:8
  1501.9 454.2 %all-gather.7 = f32[192,1,384]{2,1,0:T(1,128)S(1)} all-gather(f32[1,1,384]{2,1,0:T(1,128)S(1)} %reshape.33), channel_id=5, replica_groups=mesh['section'=48,'tensor'=4,'dp'=4] {'section','tensor'}, dimensions={0}, use_global_device_ids=true | all-gather | bytes 296448 | tf_op jit(solution)/shard_map/all_gather | solution.py:8
  1956.1 26.8 %while.21 = (s32[]{:T(128)}, f32[384]{0:T(512)S(1)}, f32[384]{0:T(512)S(1)}, f32[384]{0:T(512)S(1)}, f32[384]{0:T(512)S(1)}, /*index=5*/f32[192,384]{1,0:T(8,128...) while((s32[]{:T(128)}, f32[384]{0:T(512)S(1)}, ...), condition=%wide.region_5.6_spmd, body=%wide.region_4.5_spmd.sunk | while | flops 4613 | bytes 38567 | solution.py:13
  1983.0 0.0 copy-done
  1983.0 0.6 subtract_select_fusion
  1983.6 0.5 fusion.1
  (1160 shorter events, 19.8 us)
Async XLA Ops:
  7.2 122.7 %all-gather.10.cloned.1.call-start = ((), (), s32[]{:S(2)}) async-start(), calls=%async_computation | async-start | bytes 6422528 | tf_op jit(solution)/shard_map/all_gather | solution.py:35
  115.8 1867.2 %copy-start = (f32[8]{0:T(128)S(1)}, f32[8]{0:T(128)}, u32[]{:S(2)}) copy-start(f32[8]{0:T(128)} %param.10) | copy-start | bytes 100
Sparse Core Ops, SparseCore 0:
  22.3 107.4 all-gather.9
where the time goes:
time: 1990 us
  blocking collectives  1920 us (96%)
    all_gather x4, blocking collectives, joined(): gathered = jax.tree.map(lambda a: lax.all_gather(a, axis), part)  1810 us
    unnamed x1, blocking collectives  90.1 us
  transfers between devices with their start and end apart: 1, of which 1 were waited for; matrix products, arithmetic and copies ran while one was open for 0% of the time, Pallas kernels for 0%

commit v1 on v0

v1 whole, which is shorter than its diff:
```python
import functools

import jax
import jax.numpy as jnp
from jax import lax
from jax.experimental import pallas as pl
from jax.experimental.pallas import tpu as pltpu
from jax.sharding import Mesh, PartitionSpec as P

NY, NZ, NR = 8, 12, 3
NQ = NZ // NR
LANES = 128
CHUNK = 1024
PLANE = ("y_lo", "zq", "zr", "core", "tensor")

GROUP = (((0, 12, 24), (8, 28, 32)), ((4, 20, 36), (16, 40, 44)))


def place(y, z, core):
    y, z = y % NY, z % NZ
    return ((y % 2) * NZ * 2 + z * 2 + core) * (NY // 2) + y // 2


def fetch(x, dy, dz, dcore=0):
    pairs = [
        (place(y + dy, z + dz, c ^ dcore), place(y, z, c))
        for y in range(NY)
        for z in range(NZ)
        for c in range(2)
    ]
    return lax.ppermute(x, PLANE, pairs)


def stats_kernel(pieces, chunk, offset_ref, *refs):
    rows, (w_ref, out_ref, acc) = refs[:pieces], refs[pieces:]
    depth = w_ref.shape[0]
    for k in range(depth // chunk):
        x = jnp.concatenate([r[:, k * chunk : (k + 1) * chunk] for r in rows], axis=0)
        part = jnp.dot(x, w_ref[k * chunk : (k + 1) * chunk, :], preferred_element_type=jnp.float32)
        if k == 0:
            acc[...] = part
        else:
            acc[...] += part
    logits = acc[...]
    digits = jnp.concatenate([r[:, depth:] for r in rows], axis=0).astype(jnp.float32)
    ids = (digits[:, 2:3] * 256 + digits[:, 1:2]) * 256 + digits[:, 0:1]
    column = lax.broadcasted_iota(jnp.int32, logits.shape, 1) + offset_ref[0]
    top = jnp.max(logits, axis=1, keepdims=True)
    expo = jnp.exp(logits - top)
    total = jnp.sum(expo, axis=1, keepdims=True)
    moment = jnp.sum(expo * logits, axis=1, keepdims=True)
    hit = column == ids.astype(jnp.int32)
    picked = jnp.sum(jnp.where(hit, logits, 0.0), axis=1, keepdims=True)
    lane = lax.broadcasted_iota(jnp.int32, out_ref.shape, 1)
    low = jnp.where(lane == 0, top, total)
    high = jnp.where(lane == 2, moment, picked)
    out_ref[...] = jnp.where(lane < 2, low, high)


def stats_of(rows, weight, offset):
    count = sum(r.shape[0] for r in rows)
    depth, voc_dev = weight.shape
    return pl.pallas_call(
        functools.partial(stats_kernel, len(rows), CHUNK),
        out_shape=jax.ShapeDtypeStruct((count, LANES), jnp.float32),
        in_specs=[pl.BlockSpec(memory_space=pltpu.SMEM)]
        + [pl.BlockSpec(memory_space=pltpu.VMEM)] * (len(rows) + 1),
        out_specs=pl.BlockSpec(memory_space=pltpu.VMEM),
        scratch_shapes=[
            pltpu.VMEM((count, voc_dev), jnp.float32),
        ],
        compiler_params=pltpu.CompilerParams(vmem_limit_bytes=16 * 2**20),
        cost_estimate=pl.CostEstimate(
            flops=2 * count * depth * voc_dev,
            bytes_accessed=2 * depth * (count + voc_dev),
            transcendentals=count * voc_dev,
        ),
    )(offset, *rows, weight)


def per_device(hidden, vocab_weight, target_ids, ref_logp, response_lengths):
    row_dev, feat = hidden.shape
    voc_dev = vocab_weight.shape[1]
    y_lo, y_hi = lax.axis_index("y_lo"), lax.axis_index("tensor")
    core = lax.axis_index("core")
    z = lax.axis_index("zq") * NR + lax.axis_index("zr")
    section = (y_lo * NZ + z) * 2 + core
    n_sec, n_ten = 4 * NZ, NY // 2
    offset = ((section * n_ten + y_hi) * voc_dev).reshape(1).astype(jnp.int32)

    digits = jnp.stack([target_ids % 256, (target_ids // 256) % 256, target_ids // 65536], axis=1)
    digits = jnp.pad(digits.astype(jnp.bfloat16), ((0, 0), (0, LANES - 3)))
    block = jnp.concatenate([hidden, digits], axis=1)
    block = jnp.broadcast_to(block[None], (NQ * n_ten,) + block.shape)
    block = lax.all_to_all(block, ("zq", "tensor"), 0, 0)
    block = block.reshape(NQ, n_ten, row_dev, feat + LANES)
    pieces = [block[:, h, :, :feat] for h in range(n_ten)] + [block[:, 0, :, feat:]]
    unit = NQ * row_dev
    near = jnp.concatenate(pieces, axis=2).reshape(unit, n_ten * feat + LANES)

    near_p = fetch(near, 0, 0, 1)
    hops = []
    for dy, dz in ((1, 0), (0, 1), (0, -1), (-1, 1), (-1, -1)):
        hops.append(fetch(near, dy, dz))
    stats_a = stats_of([near, near_p], vocab_weight, offset)
    early = jnp.concatenate(hops[:2], axis=0)
    early_p = fetch(early, 0, 0, 1)
    late = jnp.concatenate(hops[2:], axis=0)
    late_p = fetch(late, 0, 0, 1)
    stats_b = stats_of([early, early_p, late], vocab_weight, offset)
    stats_c = stats_of([late_p], vocab_weight, offset)

    s = jnp.arange(n_sec, dtype=jnp.int32)
    s_core, s_z, s_y = s % 2, (s // 2) % NZ, s // (2 * NZ)
    entry = jnp.where(s_core == core, 0, 2 * NR) + ((s_y + y_lo) % 2) * NR + (s_z - z) % NR
    table = [first for c in GROUP for row in c for first in row]
    group = sum(jnp.where(entry == i, first, 0) for i, first in enumerate(table)) + s_z // NR
    stats = jnp.concatenate([stats_a[:, :4], stats_b[:, :4], stats_c[:, :4]], axis=0)
    stats = stats.reshape(n_sec, 4 * row_dev)
    choose = (group[:, None] == s[None, :]).astype(jnp.float32)
    stats = jnp.dot(choose, stats, precision=lax.Precision.HIGHEST)
    send = jnp.broadcast_to(stats[:, None, :], (n_sec, n_ten, 4 * row_dev))
    send = send.reshape(n_sec * n_ten, 1, 4 * row_dev)
    got = lax.all_to_all(send, PLANE, 0, 0).reshape(n_sec * n_ten, row_dev, 4)

    tops = got[:, :, 0]
    top = jnp.max(tops, axis=0)
    scale = jnp.exp(tops - top[None])
    total = jnp.sum(got[:, :, 1] * scale, axis=0)
    moment = jnp.sum(got[:, :, 2] * scale, axis=0)
    picked = jnp.sum(got[:, :, 3], axis=0)
    lse = top + jnp.log(total)
    logp = picked - lse
    ent = lse - moment / total
    slot = jnp.arange(row_dev, dtype=jnp.int32)
    live = (slot < response_lengths[0]).astype(jnp.float32)
    return (logp * live, ent * live, (logp - ref_logp) * live)


def solution(mesh):
    tensor, dp = mesh.shape["tensor"], mesh.shape["dp"]
    mesh = Mesh(
        mesh.devices.reshape(2, NQ, NR, 2, tensor, dp), ("y_lo", "zq", "zr", "core", "tensor", "dp")
    )
    section = ("y_lo", "zq", "zr", "core")
    rows = P(section + ("dp",))
    in_specs = (P(section + ("dp",), "tensor"), P(None, section + ("tensor",)), rows, rows, rows)
    return jax.shard_map(
        per_device, mesh=mesh, in_specs=in_specs, out_specs=(rows, rows, rows), check_vma=False
    )
```

time: 1990 us -> 139 us (0.07)
  the two profiles are of different devices: /device:TPU:26 before, /device:TPU:1 now
where the time goes in v1:
time: 139 us; the launch traced here: 138 us
  starting transfers between devices  47.8 us (34%)
  blocking collectives  39.8 us (29%)
  waiting for transfers between devices  29.8 us (21%)
  Pallas kernels  11.6 us (8%)
  local copies, waits for them, and re-layouts  5.27 us (4%)
  other arithmetic  2.38 us (2%)
  between operations  1.59 us (1%)
    all_to_all x1, blocking collectives, per_device(): block = lax.all_to_all(block, ('zq', 'tensor'), 0, 0)  39.8 us
    ppermute x8, starting transfers between devices, fetch(): return lax.ppermute(x, PLANE, pairs)  37.4 us
    all_to_all x1, waiting for transfers between devices, per_device(): got = lax.all_to_all(send, PLANE, 0, 0).reshape(n_sec * n_ten, row_dev, 4)  15.1 us
    ppermute x8, waiting for transfers between devices, fetch(): return lax.ppermute(x, PLANE, pairs)  14.6 us
    pallas_call x3, Pallas kernels, stats_of(): pl.pallas_call(functools.partial(stats_kernel, len(rows), CHUNK), out_sha...  11.6 us
    all_to_all x1, starting transfers between devices, per_device(): got = lax.all_to_all(send, PLANE, 0, 0).reshape(n_sec * n_ten, row_dev, 4)  10.4 us
    unnamed x18, local copies, waits for them, and re-layouts  4.28 us
  transfers between devices with their start and end apart: 9, of which 4 were waited for; matrix products, arithmetic and copies ran while one was open for 0% of the time, Pallas kernels for 6%

profile of v1, /device:TPU:1, one launch (start us, length us, event | category | flops | bytes accessed | tf_op | source)
XLA Modules:
  0.0 138.5 jit_solution(15442022031970868387)
XLA Ops:
  0.6 0.7 fusion.28
  1.3 0.1 copy.36
  1.4 0.8 fusion.5
  2.2 39.8 %all_to_all.10 = bf16[16,8,2176]{2,1,0:T(8,128)(2,1)S(1)} all-to-all(bf16[16,8,2176]{2,1,0:T(8,128)(2,1)S(1)} %broadcast_in_dim.70), channel_id=1, replica_groups=mesh['y_lo'=2,'zq'=4,'zr'=3,'core'=2,'tensor'=4,'dp'=4] {'zq','tensor'}, dimensions={0} | all-to-all | bytes 1114112 | tf_op jit(solution)/shard_map/all_to_all | solution.py:95
  42.2 13.3 %collective-permute-start.4 = (bf16[32,8320]{1,0:T(8,128)(2,1)S(1)}, bf16[32,8320]{1,0:T(8,128)(2,1)S(1)}, u32[]{:S(2)}, u32[]{:S(2)}) collective-permute-start(bf16[32,8320]{1,0:T(8,128)(2,1)S(1)} %constant_dynamic-update-slice_fusion.refs_0_), channel_id=1, source_target_pairs={{352,0},{368,16},{0,32},{16,48},{32,64},{48,80},{64,96},{80,112},{... | collective-permute-start | bytes 1597448 | tf_op jit(solution)/shard_map/ppermute | solution.py:31
  55.4 1.9 %collective-permute-start.5 = (bf16[32,8320]{1,0:T(8,128)(2,1)S(1)}, bf16[32,8320]{1,0:T(8,128)(2,1)S(1)}, u32[]{:S(2)}, u32[]{:S(2)}) collective-permute-start(bf16[32,8320]{1,0:T(8,128)(2,1)S(1)} %constant_dynamic-update-slice_fusion.refs_0_), channel_id=1, source_target_pairs={{428,0},{444,16},{460,32},{476,48},{492,64},{508,80},{524,96},{540... | collective-permute-start | bytes 1597448 | tf_op jit(solution)/shard_map/ppermute | solution.py:31
  57.4 3.8 %collective-permute-start.6 = (bf16[32,8320]{1,0:T(8,128)(2,1)S(1)}, bf16[32,8320]{1,0:T(8,128)(2,1)S(1)}, u32[]{:S(2)}, u32[]{:S(2)}) collective-permute-start(bf16[32,8320]{1,0:T(8,128)(2,1)S(1)} %constant_dynamic-update-slice_fusion.refs_0_), channel_id=1, source_target_pairs={{748,0},{764,16},{396,32},{412,48},{428,64},{444,80},{460,96},{476... | collective-permute-start | bytes 1597448 | tf_op jit(solution)/shard_map/ppermute | solution.py:31
  61.2 3.9 %collective-permute-start.1 = (bf16[32,8320]{1,0:T(8,128)(2,1)S(1)}, bf16[32,8320]{1,0:T(8,128)(2,1)S(1)}, u32[]{:S(2)}, u32[]{:S(2)}) collective-permute-start(bf16[32,8320]{1,0:T(8,128)(2,1)S(1)} %constant_dynamic-update-slice_fusion.refs_0_), channel_id=1, source_target_pairs={{384,0},{400,16},{416,32},{432,48},{448,64},{464,80},{480,96},{496... | collective-permute-start | bytes 1597448 | tf_op jit(solution)/shard_map/ppermute | solution.py:31
  65.1 3.0 %collective-permute-start.2 = (bf16[32,8320]{1,0:T(8,128)(2,1)S(1)}, bf16[32,8320]{1,0:T(8,128)(2,1)S(1)}, u32[]{:S(2)}, u32[]{:S(2)}) collective-permute-start(bf16[32,8320]{1,0:T(8,128)(2,1)S(1)} %constant_dynamic-update-slice_fusion.refs_0_), channel_id=1, source_target_pairs={{32,0},{48,16},{64,32},{80,48},{96,64},{112,80},{128,96},{144,112}... | collective-permute-start | bytes 1597448 | tf_op jit(solution)/shard_map/ppermute | solution.py:31
  68.2 0.0 collective-permute-done.4
  68.2 11.7 %collective-permute-done.5 = bf16[32,8320]{1,0:T(8,128)(2,1)S(1)} collective-permute-done((bf16[32,8320]{1,0:T(8,128)(2,1)S(1)}, bf16[32,8320]{1,0:T(8,128)(2,1)S(1)}, u32[]{:S(2)}, u32[]{:S(2)}) %collective-permute-start.5) | collective-permute-done | bytes 532512 | tf_op jit(solution)/shard_map/ppermute | solution.py:31
  80.0 1.0 collective-permute-done.6
  81.0 6.4 %collective-permute-start.7 = (bf16[96,8320]{1,0:T(8,128)(2,1)S(1)}, bf16[96,8320]{1,0:T(8,128)(2,1)}, u32[]{:S(2)}, u32[]{:S(2)}) collective-permute-start(bf16[96,8320]{1,0:T(8,128)(2,1)S(1)} %constant_dynamic-update-slice_fusion.3.refs_2_), channel_id=1, source_target_pairs={{16,0},{0,16},{48,32},{32,48},{80,64},{64,80},{112,96},{96,112},{1... | collective-permute-start | bytes 4792328 | tf_op jit(solution)/shard_map/ppermute | solution.py:31
  87.4 0.0 collective-permute-done.1
  87.4 0.0 collective-permute-done.2
  87.5 3.1 %collective-permute-start.3 = (bf16[64,8320]{1,0:T(8,128)(2,1)S(1)}, bf16[64,8320]{1,0:T(8,128)(2,1)}, u32[]{:S(2)}, u32[]{:S(2)}) collective-permute-start(bf16[64,8320]{1,0:T(8,128)(2,1)S(1)} %constant_dynamic-update-slice_fusion.1.refs_0_), channel_id=1, source_target_pairs={{16,0},{0,16},{48,32},{32,48},{80,64},{64,80},{112,96},{96,112},{1... | collective-permute-start | bytes 3194888 | tf_op jit(solution)/shard_map/ppermute | solution.py:31
  90.6 1.9 %collective-permute-start = (bf16[32,8320]{1,0:T(8,128)(2,1)S(1)}, bf16[32,8320]{1,0:T(8,128)(2,1)}, u32[]{:S(2)}, u32[]{:S(2)}) collective-permute-start(bf16[32,8320]{1,0:T(8,128)(2,1)S(1)} %constant_dynamic-update-slice_fusion.refs_0_), channel_id=1, source_target_pairs={{16,0},{0,16},{48,32},{32,48},{80,64},{64,80},{112,96},{96,112},{1... | collective-permute-start | bytes 1597448 | tf_op jit(solution)/shard_map/ppermute | solution.py:31
  92.6 2.0 %collective-permute-done.refs_1_ = bf16[32,8320]{1,0:T(8,128)(2,1)} collective-permute-done((bf16[32,8320]{1,0:T(8,128)(2,1)S(1)}, bf16[32,8320]{1,0:T(8,128)(2,1)}, u32[]{:S(2)}, u32[]{:S(2)}) %collective-permute-start) | collective-permute-done | bytes 532512 | tf_op jit(solution)/shard_map/ppermute | solution.py:31
  94.6 0.0 copy-start
  94.6 4.0 %copy-done = bf16[8192,640]{1,0:T(8,128)(2,1)S(1)} copy-done((bf16[8192,640]{1,0:T(8,128)(2,1)S(1)}, bf16[8192,640]{1,0:T(8,128)(2,1)}, u32[]{:S(2)}) %copy-start) | copy-done | bytes 10485784
  98.6 0.0 slice-start
  98.6 0.0 slice-start.1
  98.6 3.4 %shard_map.76 = f32[64,128]{1,0:T(8,128)S(1)} custom-call(s32[1]{0:T(128)} %bitcast.1.offset_ref, bf16[32,8320]{1,0:T(8,128)(2,1)S(1)} %constant_dynamic-update-slice_fusion.refs_0_, bf16[32,8320]{1,0:T(8,128)(2,1)} %collective-permute-done.refs_1_, bf16[8192,640]{1,0:T(8,128)(2,1)S(1)} %copy-done), custom_call_target="tpu_custom_call" | custom-call | flops 671088640 | bytes 11534336 | tf_op jit(solution)/shard_map/pallas_call | solution.py:63
  102.0 0.0 slice-start.2
  102.0 0.0 collective-permute-done.3.refs_1_
  102.0 4.7 %shard_map.77 = f32[224,128]{1,0:T(8,128)S(1)} custom-call(s32[1]{0:T(128)} %bitcast.1.offset_ref, bf16[64,8320]{1,0:T(8,128)(2,1)S(1)} %constant_dynamic-update-slice_fusion.1.refs_0_, bf16[64,8320]{1,0:T(8,128)(2,1)} %collective-permute-done.3.refs_1_, bf16[96,8320]{1,0:T(8,128)(2,1)S(1)} %constant_dynamic-update-slice_fusion.3.refs_2_, ...), custom_call_target="tpu_custom_call" | custom-call | flops 2348810240 | bytes 14155776 | tf_op jit(solution)/shard_map/pallas_call | solution.py:63
  106.7 0.0 copy-start.1
  106.7 0.0 collective-permute-done.7.refs_0_
  106.7 0.0 slice-done
  106.7 0.0 slice-done.1
  106.7 0.0 slice-done.2
  106.8 3.6 %shard_map.78 = f32[96,128]{1,0:T(8,128)S(1)} custom-call(s32[1]{0:T(128)} %bitcast.1.offset_ref, bf16[96,8320]{1,0:T(8,128)(2,1)} %collective-permute-done.7.refs_0_, bf16[8192,640]{1,0:T(8,128)(2,1)S(1)} %bitcast.58), custom_call_target="tpu_custom_call" | custom-call | flops 1006632960 | bytes 12058624 | tf_op jit(solution)/shard_map/pallas_call | solution.py:63
  110.4 0.1 reshape.136
  110.5 0.2 fusion.6
  110.7 0.7 broadcast_in_dim.71
  111.3 10.4 %all-to-all-start.1 = ((f32[192,1,32]{2,1,0:T(1,128)}), f32[192,1,32]{2,1,0:T(1,128)S(1)}, u32[]{:S(2)}, u32[]{:S(2)}) async-start(f32[192,1,32]{2,1,0:T(1,128)} %bitcast.12), calls=%async_computation.1 | async-start | bytes 196608 | tf_op jit(solution)/shard_map/all_to_all | solution.py:124
  122.4 15.1 %all-to-all-done.1 = f32[192,1,32]{2,1,0:T(1,128)S(1)} async-done(((f32[192,1,32]{2,1,0:T(1,128)}), f32[192,1,32]{2,1,0:T(1,128)S(1)}, u32[]{:S(2)}, u32[]{:S(2)}) %all-to-all-start.1) | async-done | bytes 24608 | tf_op jit(solution)/shard_map/all_to_all | solution.py:124
  137.5 0.1 copy.30
  137.6 0.2 fusion.35
  137.7 0.2 fusion.10
  137.9 0.0 copy-done.1
  137.9 0.5 subtract_select_fusion
  (16 shorter events, 0.4 us)
Async XLA Ops:
  42.2 26.0 %collective-permute-start.4 = (bf16[32,8320]{1,0:T(8,128)(2,1)S(1)}, bf16[32,8320]{1,0:T(8,128)(2,1)S(1)}, u32[]{:S(2)}, u32[]{:S(2)}) collective-permute-start(bf16[32,8320]{1,0:T(8,128)(2,1)S(1)} %constant_dynamic-update-slice_fusion.refs_0_), channel_id=1, source_target_pairs={{352,0},{368,16},{0,32},{16,48},{32,64},{48,80},{64,96},{80,112},{... | collective-permute-start | bytes 1597448 | tf_op jit(solution)/shard_map/ppermute | solution.py:31
  55.4 24.5 %collective-permute-start.5 = (bf16[32,8320]{1,0:T(8,128)(2,1)S(1)}, bf16[32,8320]{1,0:T(8,128)(2,1)S(1)}, u32[]{:S(2)}, u32[]{:S(2)}) collective-permute-start(bf16[32,8320]{1,0:T(8,128)(2,1)S(1)} %constant_dynamic-update-slice_fusion.refs_0_), channel_id=1, source_target_pairs={{428,0},{444,16},{460,32},{476,48},{492,64},{508,80},{524,96},{540... | collective-permute-start | bytes 1597448 | tf_op jit(solution)/shard_map/ppermute | solution.py:31
  57.4 23.6 %collective-permute-start.6 = (bf16[32,8320]{1,0:T(8,128)(2,1)S(1)}, bf16[32,8320]{1,0:T(8,128)(2,1)S(1)}, u32[]{:S(2)}, u32[]{:S(2)}) collective-permute-start(bf16[32,8320]{1,0:T(8,128)(2,1)S(1)} %constant_dynamic-update-slice_fusion.refs_0_), channel_id=1, source_target_pairs={{748,0},{764,16},{396,32},{412,48},{428,64},{444,80},{460,96},{476... | collective-permute-start | bytes 1597448 | tf_op jit(solution)/shard_map/ppermute | solution.py:31
  61.2 26.2 %collective-permute-start.1 = (bf16[32,8320]{1,0:T(8,128)(2,1)S(1)}, bf16[32,8320]{1,0:T(8,128)(2,1)S(1)}, u32[]{:S(2)}, u32[]{:S(2)}) collective-permute-start(bf16[32,8320]{1,0:T(8,128)(2,1)S(1)} %constant_dynamic-update-slice_fusion.refs_0_), channel_id=1, source_target_pairs={{384,0},{400,16},{416,32},{432,48},{448,64},{464,80},{480,96},{496... | collective-permute-start | bytes 1597448 | tf_op jit(solution)/shard_map/ppermute | solution.py:31
  65.1 22.3 %collective-permute-start.2 = (bf16[32,8320]{1,0:T(8,128)(2,1)S(1)}, bf16[32,8320]{1,0:T(8,128)(2,1)S(1)}, u32[]{:S(2)}, u32[]{:S(2)}) collective-permute-start(bf16[32,8320]{1,0:T(8,128)(2,1)S(1)} %constant_dynamic-update-slice_fusion.refs_0_), channel_id=1, source_target_pairs={{32,0},{48,16},{64,32},{80,48},{96,64},{112,80},{128,96},{144,112}... | collective-permute-start | bytes 1597448 | tf_op jit(solution)/shard_map/ppermute | solution.py:31
  81.0 25.7 %collective-permute-start.7 = (bf16[96,8320]{1,0:T(8,128)(2,1)S(1)}, bf16[96,8320]{1,0:T(8,128)(2,1)}, u32[]{:S(2)}, u32[]{:S(2)}) collective-permute-start(bf16[96,8320]{1,0:T(8,128)(2,1)S(1)} %constant_dynamic-update-slice_fusion.3.refs_2_), channel_id=1, source_target_pairs={{16,0},{0,16},{48,32},{32,48},{80,64},{64,80},{112,96},{96,112},{1... | collective-permute-start | bytes 4792328 | tf_op jit(solution)/shard_map/ppermute | solution.py:31
  87.5 14.5 %collective-permute-start.3 = (bf16[64,8320]{1,0:T(8,128)(2,1)S(1)}, bf16[64,8320]{1,0:T(8,128)(2,1)}, u32[]{:S(2)}, u32[]{:S(2)}) collective-permute-start(bf16[64,8320]{1,0:T(8,128)(2,1)S(1)} %constant_dynamic-update-slice_fusion.1.refs_0_), channel_id=1, source_target_pairs={{16,0},{0,16},{48,32},{32,48},{80,64},{64,80},{112,96},{96,112},{1... | collective-permute-start | bytes 3194888 | tf_op jit(solution)/shard_map/ppermute | solution.py:31
  90.6 3.9 %collective-permute-start = (bf16[32,8320]{1,0:T(8,128)(2,1)S(1)}, bf16[32,8320]{1,0:T(8,128)(2,1)}, u32[]{:S(2)}, u32[]{:S(2)}) collective-permute-start(bf16[32,8320]{1,0:T(8,128)(2,1)S(1)} %constant_dynamic-update-slice_fusion.refs_0_), channel_id=1, source_target_pairs={{16,0},{0,16},{48,32},{32,48},{80,64},{64,80},{112,96},{96,112},{1... | collective-permute-start | bytes 1597448 | tf_op jit(solution)/shard_map/ppermute | solution.py:31
  94.6 4.0 %copy-start = (bf16[8192,640]{1,0:T(8,128)(2,1)S(1)}, bf16[8192,640]{1,0:T(8,128)(2,1)}, u32[]{:S(2)}) copy-start(bf16[8192,640]{1,0:T(8,128)(2,1)} %refs_1_.1) | copy-start | bytes 31457284
  98.6 8.1 %slice-start = ((s8[10485760]{0:T(1024)(128)(4,1)}), s8[4194304]{0:T(1024)(128)(4,1)S(1)}, s32[]{:S(2)}) async-start(s8[10485760]{0:T(1024)(128)(4,1)} %bitcast.57), calls=%async_computation.2 | async-start | bytes 8388608
  98.6 8.1 %slice-start.1 = ((s8[10485760]{0:T(1024)(128)(4,1)}), s8[4194304]{0:T(1024)(128)(4,1)S(1)}, s32[]{:S(2)}) async-start(s8[10485760]{0:T(1024)(128)(4,1)} %bitcast.57), calls=%async_computation.3 | async-start | bytes 8388608
  102.0 4.8 %slice-start.2 = ((s8[10485760]{0:T(1024)(128)(4,1)}), s8[2097152]{0:T(1024)(128)(4,1)S(1)}, s32[]{:S(2)}) async-start(s8[10485760]{0:T(1024)(128)(4,1)} %bitcast.57), calls=%async_computation.4 | async-start | bytes 4194304
  106.7 31.2 %copy-start.1 = (f32[8]{0:T(128)S(1)}, f32[8]{0:T(128)}, u32[]{:S(2)}) copy-start(f32[8]{0:T(128)} %param.8) | copy-start | bytes 100
  111.3 26.2 %all-to-all-start.1 = ((f32[192,1,32]{2,1,0:T(1,128)}), f32[192,1,32]{2,1,0:T(1,128)S(1)}, u32[]{:S(2)}, u32[]{:S(2)}) async-start(f32[192,1,32]{2,1,0:T(1,128)} %bitcast.12), calls=%async_computation.1 | async-start | bytes 196608 | tf_op jit(solution)/shard_map/all_to_all | solution.py:124

commit v2 on v1

--- a/solution.py
+++ b/solution.py
@@ -13,17 +13,15 @@
 CHUNK = 1024
 PLANE = ("y_lo", "zq", "zr", "core", "tensor")
 
-GROUP = (((0, 12, 24), (8, 28, 32)), ((4, 20, 36), (16, 40, 44)))
-
 
 def place(y, z, core):
     y, z = y % NY, z % NZ
     return ((y % 2) * NZ * 2 + z * 2 + core) * (NY // 2) + y // 2
 
 
-def fetch(x, dy, dz, dcore=0):
+def fetch(x, dz=0, across=False, swap=False):
     pairs = [
-        (place(y + dy, z + dz, c ^ dcore), place(y, z, c))
+        (place(y + (1 - 2 * c if across else 0), z + dz, c ^ swap), place(y, z, c))
         for y in range(NY)
         for z in range(NZ)
         for c in range(2)
@@ -98,23 +96,23 @@
     unit = NQ * row_dev
     near = jnp.concatenate(pieces, axis=2).reshape(unit, n_ten * feat + LANES)
 
-    near_p = fetch(near, 0, 0, 1)
-    hops = []
-    for dy, dz in ((1, 0), (0, 1), (0, -1), (-1, 1), (-1, -1)):
-        hops.append(fetch(near, dy, dz))
-    stats_a = stats_of([near, near_p], vocab_weight, offset)
-    early = jnp.concatenate(hops[:2], axis=0)
-    early_p = fetch(early, 0, 0, 1)
-    late = jnp.concatenate(hops[2:], axis=0)
-    late_p = fetch(late, 0, 0, 1)
-    stats_b = stats_of([early, early_p, late], vocab_weight, offset)
+    up = fetch(near, dz=1)
+    down = fetch(near, dz=-1)
+    side = fetch(near, across=True)
+    side_up = fetch(up, across=True)
+    side_down = fetch(down, across=True)
+    early = jnp.concatenate([near, up, down], axis=0)
+    early_p = fetch(early, swap=True)
+    stats_a = stats_of([early], vocab_weight, offset)
+    late = jnp.concatenate([side, side_up, side_down], axis=0)
+    late_p = fetch(late, swap=True)
+    stats_b = stats_of([early_p, late], vocab_weight, offset)
     stats_c = stats_of([late_p], vocab_weight, offset)
 
     s = jnp.arange(n_sec, dtype=jnp.int32)
     s_core, s_z, s_y = s % 2, (s // 2) % NZ, s // (2 * NZ)
-    entry = jnp.where(s_core == core, 0, 2 * NR) + ((s_y + y_lo) % 2) * NR + (s_z - z) % NR
-    table = [first for c in GROUP for row in c for first in row]
-    group = sum(jnp.where(entry == i, first, 0) for i, first in enumerate(table)) + s_z // NR
+    group = ((s_y + y_lo) % 2) * (n_sec // 2) + jnp.where(s_core == core, 0, n_sec // 4)
+    group = group + ((s_z - z) % NR) * NQ + s_z // NR
     stats = jnp.concatenate([stats_a[:, :4], stats_b[:, :4], stats_c[:, :4]], axis=0)
     stats = stats.reshape(n_sec, 4 * row_dev)
     choose = (group[:, None] == s[None, :]).astype(jnp.float32)

time: 139 us -> 134 us (0.964)
  starting transfers between devices: 47.8 us -> 36.9 us
  waiting for transfers between devices: 29.8 us -> 37.2 us
    ppermute x8 -> x7, starting transfers between devices: 37.4 us -> 27.8 us  [fetch(): return lax.ppermute(x, PLANE, pairs)]
    ppermute x8 -> x7, waiting for transfers between devices: 14.6 us -> 22.1 us  [fetch(): return lax.ppermute(x, PLANE, pairs)]
    unnamed x18 -> x17, local copies, waits for them, and re-layouts: 4.28 us -> 4.24 us
  transfers between devices with their start and end apart: 9 -> 8, of which waited for: 4 -> 5; matrix products, arithmetic and copies ran while one was open for 0% -> 0% of each run, Pallas kernels for 6% -> 5%
where the time goes in v2:
time: 134 us
  blocking collectives  39.8 us (30%)
  waiting for transfers between devices  37.2 us (28%)
  starting transfers between devices  36.9 us (28%)
  Pallas kernels  10.4 us (8%)
  local copies, waits for them, and re-layouts  5.18 us (4%)
  other arithmetic  2.47 us (2%)
  between operations  1.57 us (1%)
    all_to_all x1, blocking collectives, per_device(): block = lax.all_to_all(block, ('zq', 'tensor'), 0, 0)  39.8 us
    ppermute x7, starting transfers between devices, fetch(): return lax.ppermute(x, PLANE, pairs)  27.8 us
    ppermute x7, waiting for transfers between devices, fetch(): return lax.ppermute(x, PLANE, pairs)  22.1 us
    all_to_all x1, waiting for transfers between devices, per_device(): got = lax.all_to_all(send, PLANE, 0, 0).reshape(n_sec * n_ten, row_dev, 4)  15.1 us
    pallas_call x3, Pallas kernels, stats_of(): pl.pallas_call(functools.partial(stats_kernel, len(rows), CHUNK), out_sha...  10.4 us
    all_to_all x1, starting transfers between devices, per_device(): got = lax.all_to_all(send, PLANE, 0, 0).reshape(n_sec * n_ten, row_dev, 4)  9.08 us
    unnamed x17, local copies, waits for them, and re-layouts  4.24 us
  transfers between devices with their start and end apart: 8, of which 5 were waited for; matrix products, arithmetic and copies ran while one was open for 0% of the time, Pallas kernels for 5%

profile of v2, /device:TPU:1, one launch (start us, length us, event | category | flops | bytes accessed | tf_op | source)
XLA Modules:
  0.0 133.7 jit_solution(762193125595135936)
XLA Ops:
  0.6 0.7 fusion.18
  1.3 0.1 copy.36
  1.4 0.8 fusion.5
  2.2 39.8 %all_to_all.10 = bf16[16,8,2176]{2,1,0:T(8,128)(2,1)S(1)} all-to-all(bf16[16,8,2176]{2,1,0:T(8,128)(2,1)S(1)} %broadcast_in_dim.11), channel_id=1, replica_groups=mesh['y_lo'=2,'zq'=4,'zr'=3,'core'=2,'tensor'=4,'dp'=4] {'zq','tensor'}, dimensions={0} | all-to-all | bytes 1114112 | tf_op jit(solution)/shard_map/all_to_all | solution.py:93
  42.2 11.2 %collective-permute-start = (bf16[32,8320]{1,0:T(8,128)(2,1)S(1)}, bf16[32,8320]{1,0:T(8,128)(2,1)S(1)}, u32[]{:S(2)}, u32[]{:S(2)}) collective-permute-start(bf16[32,8320]{1,0:T(8,128)(2,1)S(1)} %constant_dynamic-update-slice_fusion), channel_id=1, source_target_pairs={{32,0},{48,16},{64,32},{80,48},{96,64},{112,80},{128,96},{144,112}... | collective-permute-start | bytes 1597448 | tf_op jit(solution)/shard_map/ppermute | solution.py:29
  53.3 4.0 %collective-permute-start.1 = (bf16[32,8320]{1,0:T(8,128)(2,1)S(1)}, bf16[32,8320]{1,0:T(8,128)(2,1)S(1)}, u32[]{:S(2)}, u32[]{:S(2)}) collective-permute-start(bf16[32,8320]{1,0:T(8,128)(2,1)S(1)} %constant_dynamic-update-slice_fusion), channel_id=1, source_target_pairs={{352,0},{368,16},{0,32},{16,48},{32,64},{48,80},{64,96},{80,112},{... | collective-permute-start | bytes 1597448 | tf_op jit(solution)/shard_map/ppermute | solution.py:29
  57.4 2.3 %collective-permute-start.3 = (bf16[32,8320]{1,0:T(8,128)(2,1)S(1)}, bf16[32,8320]{1,0:T(8,128)(2,1)S(1)}, u32[]{:S(2)}, u32[]{:S(2)}) collective-permute-start(bf16[32,8320]{1,0:T(8,128)(2,1)S(1)} %constant_dynamic-update-slice_fusion), channel_id=1, source_target_pairs={{384,0},{412,16},{416,32},{444,48},{448,64},{476,80},{480,96},{508... | collective-permute-start | bytes 1597448 | tf_op jit(solution)/shard_map/ppermute | solution.py:29
  59.7 6.8 %collective-permute-done = bf16[32,8320]{1,0:T(8,128)(2,1)S(1)} collective-permute-done((bf16[32,8320]{1,0:T(8,128)(2,1)S(1)}, bf16[32,8320]{1,0:T(8,128)(2,1)S(1)}, u32[]{:S(2)}, u32[]{:S(2)}) %collective-permute-start) | collective-permute-done | bytes 532512 | tf_op jit(solution)/shard_map/ppermute | solution.py:29
  66.5 2.7 %collective-permute-done.1 = bf16[32,8320]{1,0:T(8,128)(2,1)S(1)} collective-permute-done((bf16[32,8320]{1,0:T(8,128)(2,1)S(1)}, bf16[32,8320]{1,0:T(8,128)(2,1)S(1)}, u32[]{:S(2)}, u32[]{:S(2)}) %collective-permute-start.1) | collective-permute-done | bytes 532512 | tf_op jit(solution)/shard_map/ppermute | solution.py:29
  69.2 0.1 pad_maximum_fusion.refs_0_
  69.3 4.1 %collective-permute-start.2 = (bf16[96,8320]{1,0:T(8,128)(2,1)S(1)}, bf16[96,8320]{1,0:T(8,128)(2,1)}, u32[]{:S(2)}, u32[]{:S(2)}) collective-permute-start(bf16[96,8320]{1,0:T(8,128)(2,1)S(1)} %pad_maximum_fusion.refs_0_), channel_id=1, source_target_pairs={{16,0},{0,16},{48,32},{32,48},{80,64},{64,80},{112,96},{96,112},{1... | collective-permute-start | bytes 4792328 | tf_op jit(solution)/shard_map/ppermute | solution.py:29
  73.4 2.4 %collective-permute-start.4 = (bf16[32,8320]{1,0:T(8,128)(2,1)S(1)}, bf16[32,8320]{1,0:T(8,128)(2,1)S(1)}, u32[]{:S(2)}, u32[]{:S(2)}) collective-permute-start(bf16[32,8320]{1,0:T(8,128)(2,1)S(1)} %collective-permute-done), channel_id=1, source_target_pairs={{384,0},{412,16},{416,32},{444,48},{448,64},{476,80},{480,96},{508... | collective-permute-start | bytes 1597448 | tf_op jit(solution)/shard_map/ppermute | solution.py:29
  75.8 1.9 %collective-permute-start.5 = (bf16[32,8320]{1,0:T(8,128)(2,1)S(1)}, bf16[32,8320]{1,0:T(8,128)(2,1)S(1)}, u32[]{:S(2)}, u32[]{:S(2)}) collective-permute-start(bf16[32,8320]{1,0:T(8,128)(2,1)S(1)} %collective-permute-done.1), channel_id=1, source_target_pairs={{384,0},{412,16},{416,32},{444,48},{448,64},{476,80},{480,96},{508... | collective-permute-start | bytes 1597448 | tf_op jit(solution)/shard_map/ppermute | solution.py:29
  77.7 0.0 collective-permute-done.3
  77.8 6.9 %collective-permute-done.4 = bf16[32,8320]{1,0:T(8,128)(2,1)S(1)} collective-permute-done((bf16[32,8320]{1,0:T(8,128)(2,1)S(1)}, bf16[32,8320]{1,0:T(8,128)(2,1)S(1)}, u32[]{:S(2)}, u32[]{:S(2)}) %collective-permute-start.4) | collective-permute-done | bytes 532512 | tf_op jit(solution)/shard_map/ppermute | solution.py:29
  84.7 5.7 %collective-permute-done.5 = bf16[32,8320]{1,0:T(8,128)(2,1)S(1)} collective-permute-done((bf16[32,8320]{1,0:T(8,128)(2,1)S(1)}, bf16[32,8320]{1,0:T(8,128)(2,1)S(1)}, u32[]{:S(2)}, u32[]{:S(2)}) %collective-permute-start.5) | collective-permute-done | bytes 532512 | tf_op jit(solution)/shard_map/ppermute | solution.py:29
  90.4 1.9 %collective-permute-start.6 = (bf16[96,8320]{1,0:T(8,128)(2,1)S(1)}, bf16[96,8320]{1,0:T(8,128)(2,1)}, u32[]{:S(2)}, u32[]{:S(2)}) collective-permute-start(bf16[96,8320]{1,0:T(8,128)(2,1)S(1)} %constant_dynamic-update-slice_fusion.1.refs_1_), channel_id=1, source_target_pairs={{16,0},{0,16},{48,32},{32,48},{80,64},{64,80},{112,96},{96,112},{1... | collective-permute-start | bytes 4792328 | tf_op jit(solution)/shard_map/ppermute | solution.py:29
  92.4 0.0 copy-start
  92.4 4.0 %copy-done = bf16[8192,640]{1,0:T(8,128)(2,1)S(1)} copy-done((bf16[8192,640]{1,0:T(8,128)(2,1)S(1)}, bf16[8192,640]{1,0:T(8,128)(2,1)}, u32[]{:S(2)}) %copy-start) | copy-done | bytes 10485784
  96.4 0.0 slice-start
  96.4 0.0 slice-start.1
  96.4 2.1 %shard_map.76 = f32[96,128]{1,0:T(8,128)S(1)} custom-call(s32[1]{0:T(128)} %bitcast.1.offset_ref, bf16[96,8320]{1,0:T(8,128)(2,1)S(1)} %pad_maximum_fusion.refs_0_, bf16[8192,640]{1,0:T(8,128)(2,1)S(1)} %copy-done), custom_call_target="tpu_custom_call" | custom-call | flops 1006632960 | bytes 12058624 | tf_op jit(solution)/shard_map/pallas_call | solution.py:61
  98.5 0.0 slice-start.2
  98.5 0.0 collective-permute-done.2.refs_0_
  98.5 4.6 %shard_map.77 = f32[192,128]{1,0:T(8,128)S(1)} custom-call(s32[1]{0:T(128)} %bitcast.1.offset_ref, bf16[96,8320]{1,0:T(8,128)(2,1)} %collective-permute-done.2.refs_0_, bf16[96,8320]{1,0:T(8,128)(2,1)S(1)} %constant_dynamic-update-slice_fusion.1.refs_1_, bf16[8192,640]{1,0:T(8,128)(2,1)S(1)} %copy-done), custom_call_target="tpu_custom_call" | custom-call | flops 2013265920 | bytes 13631488 | tf_op jit(solution)/shard_map/pallas_call | solution.py:61
  103.2 0.0 copy-start.1
  103.2 0.0 collective-permute-done.6.refs_0_
  103.2 0.0 slice-done
  103.2 0.0 slice-done.1
  103.2 0.0 slice-done.2
  103.3 3.6 %shard_map.78 = f32[96,128]{1,0:T(8,128)S(1)} custom-call(s32[1]{0:T(128)} %bitcast.1.offset_ref, bf16[96,8320]{1,0:T(8,128)(2,1)} %collective-permute-done.6.refs_0_, bf16[8192,640]{1,0:T(8,128)(2,1)S(1)} %bitcast.58), custom_call_target="tpu_custom_call" | custom-call | flops 1006632960 | bytes 12058624 | tf_op jit(solution)/shard_map/pallas_call | solution.py:61
  106.9 0.1 reshape.105
  107.0 0.2 fusion.6
  107.2 0.7 broadcast_in_dim.12
  107.8 9.1 %all-to-all-start.1 = ((f32[192,1,32]{2,1,0:T(1,128)}), f32[192,1,32]{2,1,0:T(1,128)S(1)}, u32[]{:S(2)}, u32[]{:S(2)}) async-start(f32[192,1,32]{2,1,0:T(1,128)} %bitcast.12), calls=%async_computation.1 | async-start | bytes 196608 | tf_op jit(solution)/shard_map/all_to_all | solution.py:122
  117.6 15.1 %all-to-all-done.1 = f32[192,1,32]{2,1,0:T(1,128)S(1)} async-done(((f32[192,1,32]{2,1,0:T(1,128)}), f32[192,1,32]{2,1,0:T(1,128)S(1)}, u32[]{:S(2)}, u32[]{:S(2)}) %all-to-all-start.1) | async-done | bytes 24608 | tf_op jit(solution)/shard_map/all_to_all | solution.py:122
  132.7 0.1 copy.30
  132.8 0.2 fusion.26
  133.0 0.2 fusion.10
  133.2 0.0 copy-done.1
  133.2 0.5 subtract_select_fusion
  (14 shorter events, 0.3 us)
Async XLA Ops:
  42.2 24.4 %collective-permute-start = (bf16[32,8320]{1,0:T(8,128)(2,1)S(1)}, bf16[32,8320]{1,0:T(8,128)(2,1)S(1)}, u32[]{:S(2)}, u32[]{:S(2)}) collective-permute-start(bf16[32,8320]{1,0:T(8,128)(2,1)S(1)} %constant_dynamic-update-slice_fusion), channel_id=1, source_target_pairs={{32,0},{48,16},{64,32},{80,48},{96,64},{112,80},{128,96},{144,112}... | collective-permute-start | bytes 1597448 | tf_op jit(solution)/shard_map/ppermute | solution.py:29
  53.3 15.9 %collective-permute-start.1 = (bf16[32,8320]{1,0:T(8,128)(2,1)S(1)}, bf16[32,8320]{1,0:T(8,128)(2,1)S(1)}, u32[]{:S(2)}, u32[]{:S(2)}) collective-permute-start(bf16[32,8320]{1,0:T(8,128)(2,1)S(1)} %constant_dynamic-update-slice_fusion), channel_id=1, source_target_pairs={{352,0},{368,16},{0,32},{16,48},{32,64},{48,80},{64,96},{80,112},{... | collective-permute-start | bytes 1597448 | tf_op jit(solution)/shard_map/ppermute | solution.py:29
  57.4 20.4 %collective-permute-start.3 = (bf16[32,8320]{1,0:T(8,128)(2,1)S(1)}, bf16[32,8320]{1,0:T(8,128)(2,1)S(1)}, u32[]{:S(2)}, u32[]{:S(2)}) collective-permute-start(bf16[32,8320]{1,0:T(8,128)(2,1)S(1)} %constant_dynamic-update-slice_fusion), channel_id=1, source_target_pairs={{384,0},{412,16},{416,32},{444,48},{448,64},{476,80},{480,96},{508... | collective-permute-start | bytes 1597448 | tf_op jit(solution)/shard_map/ppermute | solution.py:29
  69.3 29.2 %collective-permute-start.2 = (bf16[96,8320]{1,0:T(8,128)(2,1)S(1)}, bf16[96,8320]{1,0:T(8,128)(2,1)}, u32[]{:S(2)}, u32[]{:S(2)}) collective-permute-start(bf16[96,8320]{1,0:T(8,128)(2,1)S(1)} %pad_maximum_fusion.refs_0_), channel_id=1, source_target_pairs={{16,0},{0,16},{48,32},{32,48},{80,64},{64,80},{112,96},{96,112},{1... | collective-permute-start | bytes 4792328 | tf_op jit(solution)/shard_map/ppermute | solution.py:29
  73.4 11.2 %collective-permute-start.4 = (bf16[32,8320]{1,0:T(8,128)(2,1)S(1)}, bf16[32,8320]{1,0:T(8,128)(2,1)S(1)}, u32[]{:S(2)}, u32[]{:S(2)}) collective-permute-start(bf16[32,8320]{1,0:T(8,128)(2,1)S(1)} %collective-permute-done), channel_id=1, source_target_pairs={{384,0},{412,16},{416,32},{444,48},{448,64},{476,80},{480,96},{508... | collective-permute-start | bytes 1597448 | tf_op jit(solution)/shard_map/ppermute | solution.py:29
  75.8 14.5 %collective-permute-start.5 = (bf16[32,8320]{1,0:T(8,128)(2,1)S(1)}, bf16[32,8320]{1,0:T(8,128)(2,1)S(1)}, u32[]{:S(2)}, u32[]{:S(2)}) collective-permute-start(bf16[32,8320]{1,0:T(8,128)(2,1)S(1)} %collective-permute-done.1), channel_id=1, source_target_pairs={{384,0},{412,16},{416,32},{444,48},{448,64},{476,80},{480,96},{508... | collective-permute-start | bytes 1597448 | tf_op jit(solution)/shard_map/ppermute | solution.py:29
  90.4 12.8 %collective-permute-start.6 = (bf16[96,8320]{1,0:T(8,128)(2,1)S(1)}, bf16[96,8320]{1,0:T(8,128)(2,1)}, u32[]{:S(2)}, u32[]{:S(2)}) collective-permute-start(bf16[96,8320]{1,0:T(8,128)(2,1)S(1)} %constant_dynamic-update-slice_fusion.1.refs_1_), channel_id=1, source_target_pairs={{16,0},{0,16},{48,32},{32,48},{80,64},{64,80},{112,96},{96,112},{1... | collective-permute-start | bytes 4792328 | tf_op jit(solution)/shard_map/ppermute | solution.py:29
  92.4 4.0 %copy-start = (bf16[8192,640]{1,0:T(8,128)(2,1)S(1)}, bf16[8192,640]{1,0:T(8,128)(2,1)}, u32[]{:S(2)}) copy-start(bf16[8192,640]{1,0:T(8,128)(2,1)} %refs_1_.3) | copy-start | bytes 31457284
  96.4 6.8 %slice-start = ((s8[10485760]{0:T(1024)(128)(4,1)}), s8[4194304]{0:T(1024)(128)(4,1)S(1)}, s32[]{:S(2)}) async-start(s8[10485760]{0:T(1024)(128)(4,1)} %bitcast.57), calls=%async_computation.2 | async-start | bytes 8388608
  96.4 6.9 %slice-start.1 = ((s8[10485760]{0:T(1024)(128)(4,1)}), s8[4194304]{0:T(1024)(128)(4,1)S(1)}, s32[]{:S(2)}) async-start(s8[10485760]{0:T(1024)(128)(4,1)} %bitcast.57), calls=%async_computation.3 | async-start | bytes 8388608
  98.5 4.7 %slice-start.2 = ((s8[10485760]{0:T(1024)(128)(4,1)}), s8[2097152]{0:T(1024)(128)(4,1)S(1)}, s32[]{:S(2)}) async-start(s8[10485760]{0:T(1024)(128)(4,1)} %bitcast.57), calls=%async_computation.4 | async-start | bytes 4194304
  103.2 30.0 %copy-start.1 = (f32[8]{0:T(128)S(1)}, f32[8]{0:T(128)}, u32[]{:S(2)}) copy-start(f32[8]{0:T(128)} %param.8) | copy-start | bytes 100
  107.8 24.9 %all-to-all-start.1 = ((f32[192,1,32]{2,1,0:T(1,128)}), f32[192,1,32]{2,1,0:T(1,128)S(1)}, u32[]{:S(2)}, u32[]{:S(2)}) async-start(f32[192,1,32]{2,1,0:T(1,128)} %bitcast.12), calls=%async_computation.1 | async-start | bytes 196608 | tf_op jit(solution)/shard_map/all_to_all | solution.py:122

commit v3 on v2

--- a/solution.py
+++ b/solution.py
@@ -103,17 +103,21 @@
     side_down = fetch(down, across=True)
     early = jnp.concatenate([near, up, down], axis=0)
     early_p = fetch(early, swap=True)
-    stats_a = stats_of([early], vocab_weight, offset)
-    late = jnp.concatenate([side, side_up, side_down], axis=0)
-    late_p = fetch(late, swap=True)
-    stats_b = stats_of([early_p, late], vocab_weight, offset)
-    stats_c = stats_of([late_p], vocab_weight, offset)
+    stats_o = stats_of([near], vocab_weight, offset)
+    stats_a = stats_of([up, down], vocab_weight, offset)
+    mid = jnp.concatenate([side, side_up], axis=0)
+    mid_p = fetch(mid, swap=True)
+    stats_b = stats_of([early_p, mid], vocab_weight, offset)
+    late_p = fetch(side_down, swap=True)
+    stats_c = stats_of([mid_p, side_down, late_p], vocab_weight, offset)
 
     s = jnp.arange(n_sec, dtype=jnp.int32)
     s_core, s_z, s_y = s % 2, (s // 2) % NZ, s // (2 * NZ)
-    group = ((s_y + y_lo) % 2) * (n_sec // 2) + jnp.where(s_core == core, 0, n_sec // 4)
-    group = group + ((s_z - z) % NR) * NQ + s_z // NR
-    stats = jnp.concatenate([stats_a[:, :4], stats_b[:, :4], stats_c[:, :4]], axis=0)
+    theirs = (s_core != core).astype(jnp.int32)
+    away = (s_z - z) % NR
+    far = jnp.where(away < 2, 24 + 8 * theirs + NQ * away, 40 + 4 * theirs)
+    group = jnp.where(s_y == y_lo, 12 * theirs + NQ * away, far) + s_z // NR
+    stats = jnp.concatenate([x[:, :4] for x in (stats_o, stats_a, stats_b, stats_c)], axis=0)
     stats = stats.reshape(n_sec, 4 * row_dev)
     choose = (group[:, None] == s[None, :]).astype(jnp.float32)
     stats = jnp.dot(choose, stats, precision=lax.Precision.HIGHEST)

time: 134 us -> 139 us (1.037)
  starting transfers between devices: 36.9 us -> 39.4 us
  Pallas kernels: 10.4 us -> 11.9 us
    ppermute x7 -> x8, starting transfers between devices: 27.8 us -> 31.1 us  [fetch(): return lax.ppermute(x, PLANE, pairs)]
    pallas_call x3 -> x4, Pallas kernels: 10.4 us -> 11.9 us  [stats_of(): pl.pallas_call(functools.partial(stats_kernel, len(rows), CHUNK), out_sha...]
    ppermute x7 -> x8, waiting for transfers between devices: 22.1 us -> 21.7 us  [fetch(): return lax.ppermute(x, PLANE, pairs)]
    unnamed x17 -> x16, local copies, waits for them, and re-layouts: 4.24 us -> 4.2 us
  transfers between devices with their start and end apart: 8 -> 9, of which waited for: 5 -> 4; matrix products, arithmetic and copies ran while one was open for 0% -> 1% of each run, Pallas kernels for 5% -> 6%
where the time goes in v3:
time: 139 us
  blocking collectives  39.8 us (29%)
  starting transfers between devices  39.4 us (28%)
  waiting for transfers between devices  36.8 us (26%)
  Pallas kernels  11.9 us (9%)
  local copies, waits for them, and re-layouts  5.14 us (4%)
  other arithmetic  3.65 us (3%)
  between operations  1.61 us (1%)
    all_to_all x1, blocking collectives, per_device(): block = lax.all_to_all(block, ('zq', 'tensor'), 0, 0)  39.8 us
    ppermute x8, starting transfers between devices, fetch(): return lax.ppermute(x, PLANE, pairs)  31.1 us
    ppermute x8, waiting for transfers between devices, fetch(): return lax.ppermute(x, PLANE, pairs)  21.7 us
    all_to_all x1, waiting for transfers between devices, per_device(): got = lax.all_to_all(send, PLANE, 0, 0).reshape(n_sec * n_ten, row_dev, 4)  15.1 us
    pallas_call x4, Pallas kernels, stats_of(): pl.pallas_call(functools.partial(stats_kernel, len(rows), CHUNK), out_sha...  11.9 us
    all_to_all x1, starting transfers between devices, per_device(): got = lax.all_to_all(send, PLANE, 0, 0).reshape(n_sec * n_ten, row_dev, 4)  8.3 us
    unnamed x16, local copies, waits for them, and re-layouts  4.2 us
  transfers between devices with their start and end apart: 9, of which 4 were waited for; matrix products, arithmetic and copies ran while one was open for 1% of the time, Pallas kernels for 6%

profile of v3, /device:TPU:1, one launch (start us, length us, event | category | flops | bytes accessed | tf_op | source)
XLA Modules:
  0.0 138.5 jit_solution(10958834261241894562)
XLA Ops:
  0.6 0.7 fusion.15
  1.3 0.1 copy.37
  1.4 0.8 fusion.5
  2.2 39.8 %all_to_all.10 = bf16[16,8,2176]{2,1,0:T(8,128)(2,1)S(1)} all-to-all(bf16[16,8,2176]{2,1,0:T(8,128)(2,1)S(1)} %broadcast_in_dim.4), channel_id=1, replica_groups=mesh['y_lo'=2,'zq'=4,'zr'=3,'core'=2,'tensor'=4,'dp'=4] {'zq','tensor'}, dimensions={0} | all-to-all | bytes 1114112 | tf_op jit(solution)/shard_map/all_to_all | solution.py:93
  42.2 13.3 %collective-permute-start.1 = (bf16[32,8320]{1,0:T(8,128)(2,1)S(1)}, bf16[32,8320]{1,0:T(8,128)(2,1)S(1)}, u32[]{:S(2)}, u32[]{:S(2)}) collective-permute-start(bf16[32,8320]{1,0:T(8,128)(2,1)S(1)} %constant_dynamic-update-slice_fusion.refs_0_), channel_id=1, source_target_pairs={{352,0},{368,16},{0,32},{16,48},{32,64},{48,80},{64,96},{80,112},{... | collective-permute-start | bytes 1597448 | tf_op jit(solution)/shard_map/ppermute | solution.py:29
  55.4 1.9 %collective-permute-start = (bf16[32,8320]{1,0:T(8,128)(2,1)S(1)}, bf16[32,8320]{1,0:T(8,128)(2,1)S(1)}, u32[]{:S(2)}, u32[]{:S(2)}) collective-permute-start(bf16[32,8320]{1,0:T(8,128)(2,1)S(1)} %constant_dynamic-update-slice_fusion.refs_0_), channel_id=1, source_target_pairs={{32,0},{48,16},{64,32},{80,48},{96,64},{112,80},{128,96},{144,112}... | collective-permute-start | bytes 1597448 | tf_op jit(solution)/shard_map/ppermute | solution.py:29
  57.4 2.3 %collective-permute-start.3 = (bf16[32,8320]{1,0:T(8,128)(2,1)S(1)}, bf16[32,8320]{1,0:T(8,128)(2,1)S(1)}, u32[]{:S(2)}, u32[]{:S(2)}) collective-permute-start(bf16[32,8320]{1,0:T(8,128)(2,1)S(1)} %constant_dynamic-update-slice_fusion.refs_0_), channel_id=1, source_target_pairs={{384,0},{412,16},{416,32},{444,48},{448,64},{476,80},{480,96},{508... | collective-permute-start | bytes 1597448 | tf_op jit(solution)/shard_map/ppermute | solution.py:29
  59.7 5.8 %collective-permute-done.1.refs_1_ = bf16[32,8320]{1,0:T(8,128)(2,1)S(1)} collective-permute-done((bf16[32,8320]{1,0:T(8,128)(2,1)S(1)}, bf16[32,8320]{1,0:T(8,128)(2,1)S(1)}, u32[]{:S(2)}, u32[]{:S(2)}) %collective-permute-start.1) | collective-permute-done | bytes 532512 | tf_op jit(solution)/shard_map/ppermute | solution.py:29
  65.5 3.8 %collective-permute-done.refs_0_ = bf16[32,8320]{1,0:T(8,128)(2,1)S(1)} collective-permute-done((bf16[32,8320]{1,0:T(8,128)(2,1)S(1)}, bf16[32,8320]{1,0:T(8,128)(2,1)S(1)}, u32[]{:S(2)}, u32[]{:S(2)}) %collective-permute-start) | collective-permute-done | bytes 532512 | tf_op jit(solution)/shard_map/ppermute | solution.py:29
  69.3 1.3 pad_maximum_fusion
  70.6 4.4 %collective-permute-start.2 = (bf16[96,8320]{1,0:T(8,128)(2,1)}, bf16[96,8320]{1,0:T(8,128)(2,1)}, u32[]{:S(2)}, u32[]{:S(2)}) collective-permute-start(bf16[96,8320]{1,0:T(8,128)(2,1)} %pad_maximum_fusion), channel_id=1, source_target_pairs={{16,0},{0,16},{48,32},{32,48},{80,64},{64,80},{112,96},{96,112},{1... | collective-permute-start | bytes 4792328 | tf_op jit(solution)/shard_map/ppermute | solution.py:29
  75.0 2.3 %collective-permute-start.6 = (bf16[32,8320]{1,0:T(8,128)(2,1)S(1)}, bf16[32,8320]{1,0:T(8,128)(2,1)S(1)}, u32[]{:S(2)}, u32[]{:S(2)}) collective-permute-start(bf16[32,8320]{1,0:T(8,128)(2,1)S(1)} %collective-permute-done.1.refs_1_), channel_id=1, source_target_pairs={{384,0},{412,16},{416,32},{444,48},{448,64},{476,80},{480,96},{508... | collective-permute-start | bytes 1597448 | tf_op jit(solution)/shard_map/ppermute | solution.py:29
  77.3 2.5 %collective-permute-start.4 = (bf16[32,8320]{1,0:T(8,128)(2,1)S(1)}, bf16[32,8320]{1,0:T(8,128)(2,1)S(1)}, u32[]{:S(2)}, u32[]{:S(2)}) collective-permute-start(bf16[32,8320]{1,0:T(8,128)(2,1)S(1)} %collective-permute-done.refs_0_), channel_id=1, source_target_pairs={{384,0},{412,16},{416,32},{444,48},{448,64},{476,80},{480,96},{508... | collective-permute-start | bytes 1597448 | tf_op jit(solution)/shard_map/ppermute | solution.py:29
  79.9 0.0 collective-permute-done.3
  79.9 12.0 %collective-permute-done.4 = bf16[32,8320]{1,0:T(8,128)(2,1)S(1)} collective-permute-done((bf16[32,8320]{1,0:T(8,128)(2,1)S(1)}, bf16[32,8320]{1,0:T(8,128)(2,1)S(1)}, u32[]{:S(2)}, u32[]{:S(2)}) %collective-permute-start.4) | collective-permute-done | bytes 532512 | tf_op jit(solution)/shard_map/ppermute | solution.py:29
  92.0 1.9 %collective-permute-start.5 = (bf16[64,8320]{1,0:T(8,128)(2,1)S(1)}, bf16[64,8320]{1,0:T(8,128)(2,1)}, u32[]{:S(2)}, u32[]{:S(2)}) collective-permute-start(bf16[64,8320]{1,0:T(8,128)(2,1)S(1)} %constant_dynamic-update-slice_fusion.1.refs_1_), channel_id=1, source_target_pairs={{16,0},{0,16},{48,32},{32,48},{80,64},{64,80},{112,96},{96,112},{1... | collective-permute-start | bytes 3194888 | tf_op jit(solution)/shard_map/ppermute | solution.py:29
  93.9 0.0 collective-permute-done.6.refs_1_
  93.9 2.4 %collective-permute-start.7 = (bf16[32,8320]{1,0:T(8,128)(2,1)S(1)}, bf16[32,8320]{1,0:T(8,128)(2,1)}, u32[]{:S(2)}, u32[]{:S(2)}) collective-permute-start(bf16[32,8320]{1,0:T(8,128)(2,1)S(1)} %collective-permute-done.6.refs_1_), channel_id=1, source_target_pairs={{16,0},{0,16},{48,32},{32,48},{80,64},{64,80},{112,96},{96,112},{1... | collective-permute-start | bytes 1597448 | tf_op jit(solution)/shard_map/ppermute | solution.py:29
  96.4 0.0 copy-start
  96.4 4.0 %copy-done = bf16[8192,640]{1,0:T(8,128)(2,1)S(1)} copy-done((bf16[8192,640]{1,0:T(8,128)(2,1)S(1)}, bf16[8192,640]{1,0:T(8,128)(2,1)}, u32[]{:S(2)}) %copy-start) | copy-done | bytes 10485784
  100.4 2.1 %shard_map.76 = f32[32,128]{1,0:T(8,128)S(1)} custom-call(s32[1]{0:T(128)} %bitcast.1.offset_ref, bf16[32,8320]{1,0:T(8,128)(2,1)S(1)} %constant_dynamic-update-slice_fusion.refs_0_, bf16[8192,640]{1,0:T(8,128)(2,1)S(1)} %copy-done), custom_call_target="tpu_custom_call" | custom-call | flops 335544320 | bytes 11010048 | tf_op jit(solution)/shard_map/pallas_call | solution.py:61
  102.5 0.0 slice-start
  102.5 0.0 slice-start.1
  102.5 2.2 %shard_map.77 = f32[64,128]{1,0:T(8,128)S(1)} custom-call(s32[1]{0:T(128)} %bitcast.1.offset_ref, bf16[32,8320]{1,0:T(8,128)(2,1)S(1)} %collective-permute-done.refs_0_, bf16[32,8320]{1,0:T(8,128)(2,1)S(1)} %collective-permute-done.1.refs_1_, bf16[8192,640]{1,0:T(8,128)(2,1)S(1)} %copy-done), custom_call_target="tpu_custom_call" | custom-call | flops 671088640 | bytes 11534336 | tf_op jit(solution)/shard_map/pallas_call | solution.py:61
  104.7 0.0 slice-start.2
  104.7 0.0 collective-permute-done.2.refs_0_
  104.7 4.2 %shard_map.78 = f32[160,128]{1,0:T(8,128)S(1)} custom-call(s32[1]{0:T(128)} %bitcast.1.offset_ref, bf16[96,8320]{1,0:T(8,128)(2,1)} %collective-permute-done.2.refs_0_, bf16[64,8320]{1,0:T(8,128)(2,1)S(1)} %constant_dynamic-update-slice_fusion.1.refs_1_, bf16[8192,640]{1,0:T(8,128)(2,1)S(1)} %copy-done), custom_call_target="tpu_custom_call" | custom-call | flops 1677721600 | bytes 13107200 | tf_op jit(solution)/shard_map/pallas_call | solution.py:61
  108.9 0.0 copy-start.1
  108.9 0.0 collective-permute-done.7.refs_2_
  108.9 0.0 collective-permute-done.5.refs_0_
  108.9 0.0 slice-done
  108.9 0.0 slice-done.1
  109.0 0.0 slice-done.2
  109.0 3.5 %shard_map.79 = f32[128,128]{1,0:T(8,128)S(1)} custom-call(s32[1]{0:T(128)} %bitcast.1.offset_ref, bf16[64,8320]{1,0:T(8,128)(2,1)} %collective-permute-done.5.refs_0_, bf16[32,8320]{1,0:T(8,128)(2,1)S(1)} %collective-permute-done.6.refs_1_, bf16[32,8320]{1,0:T(8,128)(2,1)} %collective-permute-done.7.refs_2_, bf16[8192,640]{1,0:T(8,128)(2,1)S(1)} %bitcast.59), custom_call_target="tpu_custom_call" | custom-call | flops 1342177280 | bytes 12582912 | tf_op jit(solution)/shard_map/pallas_call | solution.py:61
  112.5 0.1 reshape.100
  112.6 0.2 fusion.6
  112.8 0.7 broadcast_in_dim.5
  113.5 8.3 %all-to-all-start.1 = ((f32[192,1,32]{2,1,0:T(1,128)}), f32[192,1,32]{2,1,0:T(1,128)S(1)}, u32[]{:S(2)}, u32[]{:S(2)}) async-start(f32[192,1,32]{2,1,0:T(1,128)} %bitcast.12), calls=%async_computation.1 | async-start | bytes 196608 | tf_op jit(solution)/shard_map/all_to_all | solution.py:126
  122.4 15.1 %all-to-all-done.1 = f32[192,1,32]{2,1,0:T(1,128)S(1)} async-done(((f32[192,1,32]{2,1,0:T(1,128)}), f32[192,1,32]{2,1,0:T(1,128)S(1)}, u32[]{:S(2)}, u32[]{:S(2)}) %all-to-all-start.1) | async-done | bytes 24608 | tf_op jit(solution)/shard_map/all_to_all | solution.py:126
  137.6 0.1 copy.31
  137.6 0.2 fusion.21
  137.8 0.2 fusion.10
  138.0 0.0 copy-done.1
  138.0 0.5 subtract_select_fusion
  (13 shorter events, 0.3 us)
Async XLA Ops:
  42.2 23.3 %collective-permute-start.1 = (bf16[32,8320]{1,0:T(8,128)(2,1)S(1)}, bf16[32,8320]{1,0:T(8,128)(2,1)S(1)}, u32[]{:S(2)}, u32[]{:S(2)}) collective-permute-start(bf16[32,8320]{1,0:T(8,128)(2,1)S(1)} %constant_dynamic-update-slice_fusion.refs_0_), channel_id=1, source_target_pairs={{352,0},{368,16},{0,32},{16,48},{32,64},{48,80},{64,96},{80,112},{... | collective-permute-start | bytes 1597448 | tf_op jit(solution)/shard_map/ppermute | solution.py:29
  55.4 13.9 %collective-permute-start = (bf16[32,8320]{1,0:T(8,128)(2,1)S(1)}, bf16[32,8320]{1,0:T(8,128)(2,1)S(1)}, u32[]{:S(2)}, u32[]{:S(2)}) collective-permute-start(bf16[32,8320]{1,0:T(8,128)(2,1)S(1)} %constant_dynamic-update-slice_fusion.refs_0_), channel_id=1, source_target_pairs={{32,0},{48,16},{64,32},{80,48},{96,64},{112,80},{128,96},{144,112}... | collective-permute-start | bytes 1597448 | tf_op jit(solution)/shard_map/ppermute | solution.py:29
  57.4 22.5 %collective-permute-start.3 = (bf16[32,8320]{1,0:T(8,128)(2,1)S(1)}, bf16[32,8320]{1,0:T(8,128)(2,1)S(1)}, u32[]{:S(2)}, u32[]{:S(2)}) collective-permute-start(bf16[32,8320]{1,0:T(8,128)(2,1)S(1)} %constant_dynamic-update-slice_fusion.refs_0_), channel_id=1, source_target_pairs={{384,0},{412,16},{416,32},{444,48},{448,64},{476,80},{480,96},{508... | collective-permute-start | bytes 1597448 | tf_op jit(solution)/shard_map/ppermute | solution.py:29
  70.6 34.1 %collective-permute-start.2 = (bf16[96,8320]{1,0:T(8,128)(2,1)}, bf16[96,8320]{1,0:T(8,128)(2,1)}, u32[]{:S(2)}, u32[]{:S(2)}) collective-permute-start(bf16[96,8320]{1,0:T(8,128)(2,1)} %pad_maximum_fusion), channel_id=1, source_target_pairs={{16,0},{0,16},{48,32},{32,48},{80,64},{64,80},{112,96},{96,112},{1... | collective-permute-start | bytes 4792328 | tf_op jit(solution)/shard_map/ppermute | solution.py:29
  75.0 18.9 %collective-permute-start.6 = (bf16[32,8320]{1,0:T(8,128)(2,1)S(1)}, bf16[32,8320]{1,0:T(8,128)(2,1)S(1)}, u32[]{:S(2)}, u32[]{:S(2)}) collective-permute-start(bf16[32,8320]{1,0:T(8,128)(2,1)S(1)} %collective-permute-done.1.refs_1_), channel_id=1, source_target_pairs={{384,0},{412,16},{416,32},{444,48},{448,64},{476,80},{480,96},{508... | collective-permute-start | bytes 1597448 | tf_op jit(solution)/shard_map/ppermute | solution.py:29
  77.3 14.6 %collective-permute-start.4 = (bf16[32,8320]{1,0:T(8,128)(2,1)S(1)}, bf16[32,8320]{1,0:T(8,128)(2,1)S(1)}, u32[]{:S(2)}, u32[]{:S(2)}) collective-permute-start(bf16[32,8320]{1,0:T(8,128)(2,1)S(1)} %collective-permute-done.refs_0_), channel_id=1, source_target_pairs={{384,0},{412,16},{416,32},{444,48},{448,64},{476,80},{480,96},{508... | collective-permute-start | bytes 1597448 | tf_op jit(solution)/shard_map/ppermute | solution.py:29
  92.0 16.9 %collective-permute-start.5 = (bf16[64,8320]{1,0:T(8,128)(2,1)S(1)}, bf16[64,8320]{1,0:T(8,128)(2,1)}, u32[]{:S(2)}, u32[]{:S(2)}) collective-permute-start(bf16[64,8320]{1,0:T(8,128)(2,1)S(1)} %constant_dynamic-update-slice_fusion.1.refs_1_), channel_id=1, source_target_pairs={{16,0},{0,16},{48,32},{32,48},{80,64},{64,80},{112,96},{96,112},{1... | collective-permute-start | bytes 3194888 | tf_op jit(solution)/shard_map/ppermute | solution.py:29
  93.9 15.0 %collective-permute-start.7 = (bf16[32,8320]{1,0:T(8,128)(2,1)S(1)}, bf16[32,8320]{1,0:T(8,128)(2,1)}, u32[]{:S(2)}, u32[]{:S(2)}) collective-permute-start(bf16[32,8320]{1,0:T(8,128)(2,1)S(1)} %collective-permute-done.6.refs_1_), channel_id=1, source_target_pairs={{16,0},{0,16},{48,32},{32,48},{80,64},{64,80},{112,96},{96,112},{1... | collective-permute-start | bytes 1597448 | tf_op jit(solution)/shard_map/ppermute | solution.py:29
  96.4 4.0 %copy-start = (bf16[8192,640]{1,0:T(8,128)(2,1)S(1)}, bf16[8192,640]{1,0:T(8,128)(2,1)}, u32[]{:S(2)}) copy-start(bf16[8192,640]{1,0:T(8,128)(2,1)} %refs_3_.1) | copy-start | bytes 31457284
  102.5 6.5 %slice-start = ((s8[10485760]{0:T(1024)(128)(4,1)}), s8[4194304]{0:T(1024)(128)(4,1)S(1)}, s32[]{:S(2)}) async-start(s8[10485760]{0:T(1024)(128)(4,1)} %bitcast.58), calls=%async_computation.2 | async-start | bytes 8388608
  102.5 6.5 %slice-start.1 = ((s8[10485760]{0:T(1024)(128)(4,1)}), s8[4194304]{0:T(1024)(128)(4,1)S(1)}, s32[]{:S(2)}) async-start(s8[10485760]{0:T(1024)(128)(4,1)} %bitcast.58), calls=%async_computation.3 | async-start | bytes 8388608
  104.7 4.3 %slice-start.2 = ((s8[10485760]{0:T(1024)(128)(4,1)}), s8[2097152]{0:T(1024)(128)(4,1)S(1)}, s32[]{:S(2)}) async-start(s8[10485760]{0:T(1024)(128)(4,1)} %bitcast.58), calls=%async_computation.4 | async-start | bytes 4194304
  108.9 29.1 %copy-start.1 = (f32[8]{0:T(128)S(1)}, f32[8]{0:T(128)}, u32[]{:S(2)}) copy-start(f32[8]{0:T(128)} %param.8) | copy-start | bytes 100
  113.5 24.1 %all-to-all-start.1 = ((f32[192,1,32]{2,1,0:T(1,128)}), f32[192,1,32]{2,1,0:T(1,128)S(1)}, u32[]{:S(2)}, u32[]{:S(2)}) async-start(f32[192,1,32]{2,1,0:T(1,128)} %bitcast.12), calls=%async_computation.1 | async-start | bytes 196608 | tf_op jit(solution)/shard_map/all_to_all | solution.py:126
